TPU v7x, 32 devices: a whole 2x2x4 slice. The times are simulated.
32 devices in a mesh: section: 4 (over y, x), row: 8 (over z, core).
Axes of the slice: x: 2, y: 2, z: 4, core: 2. Of those that a mesh axis runs over, the one named last changes fastest.
Arguments:
- object_slices: float32 [4, 2, 1024, 1024], P('section', None, 'row'), may hold values from -5 to 5
- probe_spec: float32 [2, 1024, 1024], P(None, 'row'), may hold values from -5 to 5
- offsets: int32 [2, 2], replicated, may hold values from 0 to 1023
- measured: float32 [2, 1024, 1024], P(None, 'row'), may hold values from 0.2 to 3
Outputs:
- object_grad: float32 [4, 2, 1024, 1024], P('section', None, 'row')
All inputs are finite; a program needn't handle non-finite values.
Results may differ from a plain program's by a relative error of at most 0.0003.
Values sent between devices are 32-bit elements; how exact they have to be, the bound alone decides.
A program may use at most 128 MiB of HBM per device.

v0:
```python
import math

import jax
import jax.numpy as jnp
from jax import lax
from jax.sharding import PartitionSpec as P

fresnel_coef = 0.37
highest = lax.Precision.HIGHEST


def complex_mul(left, right):
    return jnp.stack(
        [left[0] * right[0] - left[1] * right[1], left[0] * right[1] + left[1] * right[0]]
    )


def conj_mul(left, right):
    return jnp.stack(
        [left[0] * right[0] + left[1] * right[1], left[1] * right[0] - left[0] * right[1]]
    )


def combine_parts(result, half_len, direction):
    first = result[..., :half_len]
    second = result[..., half_len:]
    return jnp.stack([first[0] + direction * second[1], first[1] - direction * second[0]])


def small_dft(stacked, tables, direction):
    half_len = tables[0].shape[0]
    both_tables = jnp.concatenate([tables[0], tables[1]], axis=1)
    flat = stacked.reshape(-1, half_len)
    result = jnp.dot(flat, both_tables, precision=highest)
    result = result.reshape(stacked.shape[:-1] + (2 * half_len,))
    return combine_parts(result, half_len, direction)


def forward_pass(field, tables):
    half_len = tables[0].shape[0]
    halves = field.reshape(field.shape[0], field.shape[1], field.shape[2], 2, half_len)
    spectra = small_dft(halves, tables, 1.0)
    even_part = spectra[:, :, :, 0]
    turned = complex_mul(spectra[:, :, :, 1], jnp.stack([tables[2], -tables[3]]))
    joined = jnp.stack([even_part + turned, even_part - turned], axis=3)
    return joined.reshape(joined.shape[0], joined.shape[1], joined.shape[2], 2 * half_len)


def inverse_pass(field, tables):
    half_len = tables[0].shape[0]
    first_half = field[:, :, :, :half_len]
    second_half = field[:, :, :, half_len:]
    twiddle = jnp.stack([tables[2], tables[3]])
    halves = jnp.stack(
        [first_half + second_half, complex_mul(first_half - second_half, twiddle)], axis=3
    )
    spectra = small_dft(halves, tables, -1.0)
    return spectra.reshape(spectra.shape[0], spectra.shape[1], spectra.shape[2], 2 * half_len)


def forward_columns(field, tables):
    half_len = tables[0].shape[0]
    lines = field.shape[3]
    both_tables = jnp.concatenate([tables[0], tables[1]], axis=1)
    halves = field.reshape(field.shape[0], field.shape[1], 2, half_len, lines)
    result = jnp.einsum("cwajl,jk->cwalk", halves, both_tables, precision=highest)
    spectra = combine_parts(result, half_len, 1.0)
    even_part = spectra[:, :, 0]
    turned = complex_mul(spectra[:, :, 1], jnp.stack([tables[2], -tables[3]]))
    joined = jnp.stack([even_part + turned, even_part - turned], axis=3)
    return joined.reshape(joined.shape[0], joined.shape[1], lines, 2 * half_len)


def inverse_columns(field, tables):
    half_len = tables[0].shape[0]
    lines = field.shape[3]
    both_tables = jnp.concatenate([tables[0], tables[1]], axis=1)
    first_half = field[:, :, :half_len]
    second_half = field[:, :, half_len:]
    twiddle = jnp.stack([tables[2][:, None], tables[3][:, None]])
    halves = jnp.stack(
        [first_half + second_half, complex_mul(first_half - second_half, twiddle)], axis=2
    )
    result = jnp.einsum("cwajl,jk->cwlak", halves, both_tables, precision=highest)
    spectra = combine_parts(result, half_len, -1.0)
    return spectra.reshape(spectra.shape[0], spectra.shape[1], lines, 2 * half_len)


def transform_forward(field, tables):
    partial_out = forward_pass(field, tables)

    def finish(piece):
        return forward_columns(piece, tables)

    return finish(lax.all_to_all(partial_out, "row", split_axis=3, concat_axis=2, tiled=True))


def transform_inverse(field, tables):
    partial_out = inverse_pass(field, tables)

    def finish(piece):
        return inverse_columns(piece, tables)

    return finish(lax.all_to_all(partial_out, "row", split_axis=3, concat_axis=2, tiled=True))


def section_forward(spectrum, multiplier, slab_obj, propagator, tables):
    wavefield = transform_inverse(complex_mul(spectrum, multiplier), tables)
    kept = []
    outgoing = wavefield
    for layer in range(slab_obj.shape[0]):
        kept.append(wavefield)
        outgoing = transform_forward(complex_mul(slab_obj[layer][:, None], wavefield), tables)
        if layer + 1 < slab_obj.shape[0]:
            wavefield = transform_inverse(complex_mul(outgoing, propagator), tables)
    return (outgoing, jnp.stack(kept))


def section_backward(adjoint, kept, multiplier, slab_obj, propagator, tables):
    layer_total = slab_obj.shape[0]
    grads = [None] * layer_total
    for layer in reversed(range(layer_total)):
        wave_adj = transform_inverse(adjoint, tables)
        grads[layer] = jnp.sum(conj_mul(wave_adj, kept[layer]), axis=1)
        field_adj = conj_mul(wave_adj, slab_obj[layer][:, None])
        backward_spec = transform_forward(field_adj, tables)
        if layer > 0:
            adjoint = conj_mul(backward_spec, propagator)
        else:
            adjoint = conj_mul(backward_spec, multiplier)
    return (adjoint, jnp.stack(grads))


def loss_adjoint(outgoing, target):
    power = outgoing[0] * outgoing[0] + outgoing[1] * outgoing[1]
    return 0.5 * (power - target)[None] * outgoing


def shards(object_slices, probe_spec, offsets, measured):
    line_count = object_slices.shape[2]
    width = object_slices.shape[3]
    half_len = width // 2
    wave_count = offsets.shape[0]
    section_count = lax.axis_size("section")
    section_pos = lax.axis_index("section")
    row_pos = lax.axis_index("row")
    index = jnp.arange(half_len, dtype=jnp.int32)
    product = index[:, None] * index[None, :] % half_len
    angle = 2.0 * math.pi / half_len * product.astype(jnp.float32)
    scale = 1.0 / math.sqrt(width)
    twid_angle = 2.0 * math.pi / width * index.astype(jnp.float32)
    tables = (
        jnp.cos(angle) * scale,
        jnp.sin(angle) * scale,
        jnp.cos(twid_angle),
        jnp.sin(twid_angle),
    )
    column_freq = row_pos * line_count + jnp.arange(line_count, dtype=jnp.int32)
    row_freq = jnp.arange(width, dtype=jnp.int32)
    column_signed = jnp.where(column_freq < half_len, column_freq, column_freq - width)
    row_signed = jnp.where(row_freq < half_len, row_freq, row_freq - width)
    square_sum = (
        column_signed[:, None] * column_signed[:, None] + row_signed[None, :] * row_signed[None, :]
    )
    phase = -math.pi * fresnel_coef / width * square_sum.astype(jnp.float32)
    propagator = jnp.stack([jnp.cos(phase), jnp.sin(phase)])[:, None]
    turns = (
        row_freq[None, None, :] * offsets[:, 0][:, None, None]
        + column_freq[None, :, None] * offsets[:, 1][:, None, None]
    ) % width
    ramp_angle = 2.0 * math.pi / width * turns.astype(jnp.float32)
    ramps = jnp.stack([jnp.cos(ramp_angle), -jnp.sin(ramp_angle)])
    start_spec = probe_spec[:, None]
    all_obj = lax.all_gather(object_slices, "section", axis=0, tiled=True)
    wave_pick = section_pos % wave_count
    ramp_pick = lax.dynamic_slice_in_dim(ramps, wave_pick, 1, axis=1)
    outgoing, kept = section_forward(start_spec, ramp_pick, all_obj, propagator, tables)
    target = lax.dynamic_slice_in_dim(measured, wave_pick, 1, axis=0)
    unused, grads = section_backward(
        loss_adjoint(outgoing, target), kept, ramp_pick, all_obj, propagator, tables
    )
    summed = lax.psum_scatter(grads, "section", scatter_dimension=0, tiled=True)
    return summed * (wave_count / section_count)


def solution(mesh):
    placed = (P("section", None, "row", None), P(None, "row", None), P(), P(None, "row", None))
    return jax.shard_map(
        shards,
        mesh=mesh,
        in_specs=placed,
        out_specs=P("section", None, "row", None),
        check_vma=False,
    )
```

profile of v0, /device:TPU:1, one launch (start us, length us, event | category | flops | bytes accessed | tf_op | source)
XLA Modules:
  0.0 939.0 jit_solution(7419705231135184169)
XLA Ops:
  8.4 4.2 sine_negate_fusion
  14.3 4.2 sine_multiply_fusion
  18.4 3.9 convolution_bitcast_fusion.29
  31.0 6.4 all-to-all-start
  37.4 25.7 %all-to-all-done = f32[2,1,128,1024]{2,1,0,3:T(1,128)} async-done(((f32[2,1,128,1024]{2,1,0,3:T(1,128)}), f32[2,1,128,1024]{2,1,0,3:T(1,128)}, u32[]{:S(2)}, u32[]{:S(2)}) %all-to-all-start) | async-done | bytes 1048608 | tf_op jit(solution)/shard_map/all_to_all | solution.py:104
  78.2 4.2 fusion.160
  98.8 5.3 all-to-all-start.1
  104.1 25.7 %all-to-all-done.1 = f32[2,1,128,1024]{2,0,1,3:T(2,128)} async-done(((f32[2,1,128,1024]{2,0,1,3:T(2,128)}), f32[2,1,128,1024]{2,0,1,3:T(2,128)}, u32[]{:S(2)}, u32[]{:S(2)}) %all-to-all-start.1) | async-done | bytes 1048608 | tf_op jit(solution)/shard_map/all_to_all | solution.py:95
  134.6 4.7 convolution_bitcast_fusion.26
  148.6 3.7 multiply_subtract_fusion.5
  164.7 5.3 all-to-all-start.2
  174.1 21.6 %all-to-all-done.2 = f32[2,1,128,1024]{2,1,0,3:T(1,128)} async-done(((f32[2,1,128,1024]{2,1,0,3:T(1,128)}), f32[2,1,128,1024]{2,1,0,3:T(1,128)}, u32[]{:S(2)}, u32[]{:S(2)}) %all-to-all-start.2) | async-done | bytes 1048608 | tf_op jit(solution)/shard_map/all_to_all | solution.py:104
  222.3 29.3 %all_to_all.249 = f32[2,1,128,1024]{2,0,1,3:T(2,128)S(1)} all-to-all(f32[2,1,128,1024]{2,0,1,3:T(2,128)S(1)} %copy.466), channel_id=1, replica_groups=mesh['section'=4,'row'=8] {'row'}, dimensions={3} | all-to-all | bytes 2097152 | tf_op jit(solution)/shard_map/all_to_all | solution.py:95
  255.3 4.7 convolution_bitcast_fusion.22
  269.5 3.7 multiply_subtract_fusion.4
  285.6 5.4 all-to-all-start.4
  295.2 21.5 %all-to-all-done.4 = f32[2,1,128,1024]{2,1,0,3:T(1,128)} async-done(((f32[2,1,128,1024]{2,1,0,3:T(1,128)}), f32[2,1,128,1024]{2,1,0,3:T(1,128)}, u32[]{:S(2)}, u32[]{:S(2)}) %all-to-all-start.4) | async-done | bytes 1048608 | tf_op jit(solution)/shard_map/all_to_all | solution.py:104
  343.4 29.1 %all_to_all.250 = f32[2,1,128,1024]{2,0,1,3:T(2,128)S(1)} all-to-all(f32[2,1,128,1024]{2,0,1,3:T(2,128)S(1)} %copy.489), channel_id=1, replica_groups=mesh['section'=4,'row'=8] {'row'}, dimensions={3} | all-to-all | bytes 2097152 | tf_op jit(solution)/shard_map/all_to_all | solution.py:95
  376.2 4.7 convolution_bitcast_fusion.18
  406.6 5.6 all-to-all-start.6
  416.4 21.5 %all-to-all-done.6 = f32[2,1,128,1024]{2,1,0,3:T(1,128)} async-done(((f32[2,1,128,1024]{2,1,0,3:T(1,128)}), f32[2,1,128,1024]{2,1,0,3:T(1,128)}, u32[]{:S(2)}, u32[]{:S(2)}) %all-to-all-start.6) | async-done | bytes 1048608 | tf_op jit(solution)/shard_map/all_to_all | solution.py:104
  465.4 5.3 all-to-all-start.7
  473.6 22.8 %all-to-all-done.7 = f32[2,1,128,1024]{2,0,1,3:T(2,128)} async-done(((f32[2,1,128,1024]{2,0,1,3:T(2,128)}), f32[2,1,128,1024]{2,0,1,3:T(2,128)}, u32[]{:S(2)}, u32[]{:S(2)}) %all-to-all-start.7) | async-done | bytes 1048608 | tf_op jit(solution)/shard_map/all_to_all | solution.py:95
  527.1 29.1 %all_to_all.251 = f32[2,1,128,1024]{2,1,0,3:T(1,128)S(1)} all-to-all(f32[2,1,128,1024]{2,1,0,3:T(1,128)S(1)} %copy.526), channel_id=1, replica_groups=mesh['section'=4,'row'=8] {'row'}, dimensions={3} | all-to-all | bytes 2097152 | tf_op jit(solution)/shard_map/all_to_all | solution.py:104
  574.4 29.4 %all_to_all.252 = f32[2,1,128,1024]{2,0,1,3:T(2,128)S(1)} all-to-all(f32[2,1,128,1024]{2,0,1,3:T(2,128)S(1)} %copy.536), channel_id=1, replica_groups=mesh['section'=4,'row'=8] {'row'}, dimensions={3} | all-to-all | bytes 2097152 | tf_op jit(solution)/shard_map/all_to_all | solution.py:95
  626.6 29.2 %all_to_all.253 = f32[2,1,128,1024]{2,1,0,3:T(1,128)S(1)} all-to-all(f32[2,1,128,1024]{2,1,0,3:T(1,128)S(1)} %copy.548), channel_id=1, replica_groups=mesh['section'=4,'row'=8] {'row'}, dimensions={3} | all-to-all | bytes 2097152 | tf_op jit(solution)/shard_map/all_to_all | solution.py:104
  676.4 29.2 %all_to_all.254 = f32[2,1,128,1024]{2,0,1,3:T(2,128)S(1)} all-to-all(f32[2,1,128,1024]{2,0,1,3:T(2,128)S(1)} %copy.558), channel_id=1, replica_groups=mesh['section'=4,'row'=8] {'row'}, dimensions={3} | all-to-all | bytes 2097152 | tf_op jit(solution)/shard_map/all_to_all | solution.py:95
  728.2 29.4 %all_to_all.255 = f32[2,1,128,1024]{2,1,0,3:T(1,128)S(1)} all-to-all(f32[2,1,128,1024]{2,1,0,3:T(1,128)S(1)} %copy.570), channel_id=1, replica_groups=mesh['section'=4,'row'=8] {'row'}, dimensions={3} | all-to-all | bytes 2097152 | tf_op jit(solution)/shard_map/all_to_all | solution.py:104
  778.2 29.2 %all_to_all.256 = f32[2,1,128,1024]{2,0,1,3:T(2,128)S(1)} all-to-all(f32[2,1,128,1024]{2,0,1,3:T(2,128)S(1)} %copy.580), channel_id=1, replica_groups=mesh['section'=4,'row'=8] {'row'}, dimensions={3} | all-to-all | bytes 2097152 | tf_op jit(solution)/shard_map/all_to_all | solution.py:95
  832.1 5.2 all-to-all-start.14
  843.0 19.9 %all-to-all-done.14 = f32[2,1,128,1024]{2,1,0,3:T(1,128)} async-done(((f32[2,1,128,1024]{2,1,0,3:T(1,128)}), f32[2,1,128,1024]{2,1,0,3:T(1,128)}, u32[]{:S(2)}, u32[]{:S(2)}) %all-to-all-start.14) | async-done | bytes 1048608 | tf_op jit(solution)/shard_map/all_to_all | solution.py:104
  877.5 51.8 %reduce-scatter.4.cloned.1.call-done = f32[1,2,128,1024]{2,3,1,0:T(8,128)} async-done(((f32[4,2,128,1024]{2,3,1,0:T(8,128)}), f32[1,2,128,1024]{2,3,1,0:T(8,128)}) %reduce-scatter.4.cloned.1.call-update) | async-done | bytes 1048592
  (386 shorter events, 402.7 us)
Async XLA Ops:
  6.5 464.1 %copy-start = (f32[2,128,1024]{2,1,0:T(8,128)S(1)}, f32[2,128,1024]{2,1,0:T(8,128)}, u32[]{:S(2)}) copy-start(f32[2,128,1024]{2,1,0:T(8,128)} %param.7) | copy-start | bytes 3145732
  6.5 71.7 %all-gather.2.cloned.1.call-start = ((), (), s32[]{:S(2)}) async-start(), calls=%async_computation.16 | async-start | bytes 5242880 | tf_op jit(solution)/shard_map/all_gather | solution.py:174
  31.0 32.1 %all-to-all-start = ((f32[2,1,128,1024]{2,1,0,3:T(1,128)}), f32[2,1,128,1024]{2,1,0,3:T(1,128)}, u32[]{:S(2)}, u32[]{:S(2)}) async-start(f32[2,1,128,1024]{2,1,0,3:T(1,128)} %copy.432), calls=%async_computation | async-start | bytes 2097152 | tf_op jit(solution)/shard_map/all_to_all | solution.py:104
  98.8 31.0 %all-to-all-start.1 = ((f32[2,1,128,1024]{2,0,1,3:T(2,128)}), f32[2,1,128,1024]{2,0,1,3:T(2,128)}, u32[]{:S(2)}, u32[]{:S(2)}) async-start(f32[2,1,128,1024]{2,0,1,3:T(2,128)} %copy.443), calls=%async_computation.1 | async-start | bytes 2097152 | tf_op jit(solution)/shard_map/all_to_all | solution.py:95
  164.7 31.0 %all-to-all-start.2 = ((f32[2,1,128,1024]{2,1,0,3:T(1,128)}), f32[2,1,128,1024]{2,1,0,3:T(1,128)}, u32[]{:S(2)}, u32[]{:S(2)}) async-start(f32[2,1,128,1024]{2,1,0,3:T(1,128)} %copy.455), calls=%async_computation.2 | async-start | bytes 2097152 | tf_op jit(solution)/shard_map/all_to_all | solution.py:104
  285.6 31.1 %all-to-all-start.4 = ((f32[2,1,128,1024]{2,1,0,3:T(1,128)}), f32[2,1,128,1024]{2,1,0,3:T(1,128)}, u32[]{:S(2)}, u32[]{:S(2)}) async-start(f32[2,1,128,1024]{2,1,0,3:T(1,128)} %copy.478), calls=%async_computation.4 | async-start | bytes 2097152 | tf_op jit(solution)/shard_map/all_to_all | solution.py:104
  406.6 31.3 %all-to-all-start.6 = ((f32[2,1,128,1024]{2,1,0,3:T(1,128)}), f32[2,1,128,1024]{2,1,0,3:T(1,128)}, u32[]{:S(2)}, u32[]{:S(2)}) async-start(f32[2,1,128,1024]{2,1,0,3:T(1,128)} %copy.501), calls=%async_computation.6 | async-start | bytes 2097152 | tf_op jit(solution)/shard_map/all_to_all | solution.py:104
  465.4 31.0 %all-to-all-start.7 = ((f32[2,1,128,1024]{2,0,1,3:T(2,128)}), f32[2,1,128,1024]{2,0,1,3:T(2,128)}, u32[]{:S(2)}, u32[]{:S(2)}) async-start(f32[2,1,128,1024]{2,0,1,3:T(2,128)} %copy.512), calls=%async_computation.7 | async-start | bytes 2097152 | tf_op jit(solution)/shard_map/all_to_all | solution.py:95
  506.1 6.3 copy-start.20
  564.0 3.0 copy-start.14
  565.4 1.6 copy-start.15
  662.2 5.4 copy-start.12
  662.3 5.4 copy-start.13
  764.1 5.3 copy-start.6
  764.1 5.3 copy-start.7
  830.0 7.2 copy-start.10
  830.0 7.2 copy-start.11
  832.1 30.9 %all-to-all-start.14 = ((f32[2,1,128,1024]{2,1,0,3:T(1,128)}), f32[2,1,128,1024]{2,1,0,3:T(1,128)}, u32[]{:S(2)}, u32[]{:S(2)}) async-start(f32[2,1,128,1024]{2,1,0,3:T(1,128)} %copy.592), calls=%async_computation.14 | async-start | bytes 2097152 | tf_op jit(solution)/shard_map/all_to_all | solution.py:104
  837.2 92.1 %reduce-scatter.4.cloned.1.call-start = ((), (), s32[]{:S(2)}) async-start(), calls=%async_computation.17 | async-start | bytes 5242880
  837.2 2.6 copy-start.8
  837.3 2.6 copy-start.9
  837.3 2.6 copy-start.16
  837.3 2.6 copy-start.17
  839.8 1.4 copy-start.4
  839.9 1.6 copy-start.18
  839.9 1.9 copy-start.19
  870.7 2.2 copy-start.2
  870.7 2.2 copy-start.3
  873.0 1.6 copy-start.21
  873.0 1.9 copy-start.22
  873.0 2.2 copy-start.23
  877.5 54.4 %copy-start.1 = (f32[2,128,1024]{2,1,0:T(8,128)S(1)}, f32[2,128,1024]{2,1,0:T(8,128)}, u32[]{:S(2)}) copy-start(f32[2,128,1024]{2,1,0:T(8,128)} %param.7) | copy-start | bytes 3145732
  (2 other events, 2.6 us)
Sparse Core Ops, SparseCore 0:
  9.2 54.4 all-gather.1
  877.6 51.6 reduce-scatter.3
where the time goes:
time: 954 us; the launch traced here: 939 us
  blocking collectives  234 us (25%)
  local copies, waits for them, and re-layouts  226 us (24%)
  waiting for transfers between devices  211 us (22%)
  matrix products  111 us (12%)
  other arithmetic  103 us (11%)
  starting transfers between devices  38.5 us (4%)
  between operations  15.4 us (2%)
    all_to_all x5, blocking collectives, transform_forward(): lax.all_to_all(partial_out, 'row', split_axis=3, concat_axis=2, tiled=True)  146 us
    all_to_all x5, waiting for transfers between devices, transform_inverse(): lax.all_to_all(partial_out, 'row', split_axis=3, concat_axis=2, tiled=True)  110 us
    all_to_all x3, blocking collectives, transform_inverse(): lax.all_to_all(partial_out, 'row', split_axis=3, concat_axis=2, tiled=True)  87.7 us
    dot_general x15, matrix products, small_dft(): result = jnp.dot(flat, both_tables, precision=highest)  53.8 us
    unnamed x3, waiting for transfers between devices  52.5 us
    all_to_all x2, waiting for transfers between devices, transform_forward(): lax.all_to_all(partial_out, 'row', split_axis=3, concat_axis=2, tiled=True)  48.5 us
    all_to_all x16, local copies, waits for them, and re-layouts, transform_inverse(): lax.all_to_all(partial_out, 'row', split_axis=3, concat_axis=2, tiled=True)  30.8 us
    dot_general x8, matrix products, inverse_columns(): jnp.einsum('cwajl,jk->cwlak', halves, both_tables, precision=highest)  28.8 us
  transfers between devices with their start and end apart: 9, of which 8 were waited for; matrix products, arithmetic and copies ran while one was open for 6% of the time, Pallas kernels for 0%

commit v1 on v0

--- a/solution.py
+++ b/solution.py
@@ -2,7 +2,10 @@
 
 import jax
 import jax.numpy as jnp
+import numpy as np
 from jax import lax
+from jax.experimental import pallas as pl
+from jax.experimental.pallas import tpu as pltpu
 from jax.sharding import PartitionSpec as P
 
 fresnel_coef = 0.37
@@ -183,12 +186,449 @@
     return summed * (wave_count / section_count)
 
 
+def split_table(table):
+    both = np.concatenate([table.real, table.imag], axis=-1).astype(np.float32)
+    high = both.astype(jnp.bfloat16)
+    low = (both - high.astype(np.float32)).astype(jnp.bfloat16)
+    return high, low
+
+
+def fused_tables(width):
+    half, quarter = width // 2, width // 4
+    freq = np.arange(width)
+    signed = np.where(freq < half, freq, freq - width).astype(np.float64)
+    response = np.exp(-1j * np.pi * fresnel_coef / width * signed * signed)
+    place = np.arange(quarter)
+    place = np.where(place < quarter // 2, 2 * place, 2 * (place - quarter // 2) + 1)
+    gap = place[None, :] - place[:, None]
+    circ = []
+    for turn in range(4):
+        line = np.zeros(width, np.complex128)
+        line[turn::4] = response[turn::4]
+        kernel = np.fft.ifft(line)
+        circ.append(kernel[gap % width])
+    index = np.arange(half)
+    even = np.exp(-2j * np.pi * (2 * index[:, None] * index[None, :] % width) / width)
+    odd = np.exp(-2j * np.pi * ((2 * index[:, None] + 1) * index[None, :] % width) / width)
+    scale = 1.0 / math.sqrt(width)
+    dft = np.stack([even, odd, odd.T]) * scale
+    return split_table(np.stack(circ)) + split_table(dft)
+
+
+def dot_split(left, high, low):
+    left_high = left.astype(jnp.bfloat16)
+    left_low = (left - left_high.astype(jnp.float32)).astype(jnp.bfloat16)
+    out = jnp.dot(left_low, high, preferred_element_type=jnp.float32)
+    out += jnp.dot(left_high, low, preferred_element_type=jnp.float32)
+    return out + jnp.dot(left_high, high, preferred_element_type=jnp.float32)
+
+
+def complex_dot(left, high, low):
+    out = dot_split(left, high, low)
+    lines, width = out.shape[0] // 2, out.shape[1] // 2
+    real = out[:lines, :width] - out[lines:, width:]
+    imag = out[:lines, width:] + out[lines:, :width]
+    return jnp.concatenate([real, imag], axis=0)
+
+
+def times_i(value):
+    lines = value.shape[0] // 2
+    return jnp.concatenate([-value[lines:], value[:lines]], axis=0)
+
+
+def fused_kernel(
+    dims, obj_ref, spec_ref, meas_ref, ramp_y, ramp_x, circ_h, circ_l, dft_h, dft_l, out_ref,
+    state, send, recv, spec_in, meas_out, meas_in, obj_out, obj_row, obj_col, kept, grad_out,
+    grad_row, grad_col, send_sem, recv_sem, spec_sem, meas_sem, obj_send, obj_sem, grad_send,
+    grad_sem,
+):
+    sections, rows, waves, layers, width = dims
+    wave_rows = rows // waves
+    group = sections * wave_rows
+    lines = width // group
+    shard = width // rows
+    per = shard // lines
+    half, chunk = width // 2, width // 8
+    sec = lax.axis_index("section")
+    row = lax.axis_index("row")
+    wave = row // wave_rows
+    mine = (row % wave_rows) * sections + sec
+    total = sections * rows
+    me = sec * rows + row
+
+    def place(of_wave, member):
+        return member % sections, of_wave * wave_rows + member // sections
+
+    def push(src, dst, sent, got, to_sec, to_row):
+        home = jnp.logical_and(to_sec == sec, to_row == row)
+
+        @pl.when(home)
+        def _():
+            pltpu.make_async_copy(src, dst, got).start()
+
+        @pl.when(jnp.logical_not(home))
+        def _():
+            pltpu.make_async_remote_copy(
+                src_ref=src, dst_ref=dst, send_sem=sent, recv_sem=got,
+                device_id=(to_sec, to_row), device_id_type=pl.DeviceIdType.MESH,
+            ).start()
+
+    def settle(src, sent, to_sec, to_row):
+        @pl.when(jnp.logical_not(jnp.logical_and(to_sec == sec, to_row == row)))
+        def _():
+            pltpu.make_async_copy(src, src, sent).wait()
+
+    barrier = pltpu.get_barrier_semaphore()
+
+    def greet(step, carry):
+        other = (me + step) % total
+        pl.semaphore_signal(
+            barrier, inc=1, device_id=(other // rows, other % rows),
+            device_id_type=pl.DeviceIdType.MESH,
+        )
+        return carry
+
+    lax.fori_loop(1, total, greet, 0)
+    pl.semaphore_wait(barrier, total - 1)
+
+    spec_wave = sec // per
+    spec_part = sec % per
+    spec_to = place(spec_wave, row * per + spec_part)
+    spec_src = spec_ref.at[:, pl.ds(pl.multiple_of(spec_part * lines, lines), lines)]
+    push(spec_src, spec_in, spec_sem.at[0], spec_sem.at[1], *spec_to)
+
+    def obj_row_push(layer, act):
+        for part in range(per):
+            for of_wave in range(waves):
+                src = obj_ref.at[:, pl.ds(part * lines, lines)]
+                to = place(of_wave, row * per + part)
+                if act:
+                    push(src, obj_row.at[layer // 2], obj_send.at[0], obj_sem.at[layer], *to)
+                else:
+                    settle(src, obj_send.at[0], *to)
+
+    def obj_col_push(layer, act):
+        def step(count, carry):
+            member = count // waves
+            of_wave = count % waves
+            to = place(of_wave, member)
+            src = obj_out.at[member]
+            if act:
+                push(src, obj_col.at[layer // 2, row], obj_send.at[0], obj_sem.at[layer], *to)
+            else:
+                settle(src, obj_send.at[0], *to)
+            return carry
+
+        lax.fori_loop(0, group * waves, step, 0)
+
+    def transpose_obj():
+        for block in range(width // shard):
+            for part in range(2):
+                turned = obj_ref[part, :, block * shard:(block + 1) * shard].T
+                for piece in range(per):
+                    obj_out[block * per + piece, :, part * shard:(part + 1) * shard] = (
+                        turned[piece * lines:(piece + 1) * lines]
+                    )
+
+    for layer in range(layers):
+        @pl.when(sec == layer)
+        def _(layer=layer):
+            if layer % 2 == 0:
+                obj_row_push(layer, True)
+            else:
+                transpose_obj()
+                obj_col_push(layer, True)
+
+    span = width // sections
+    for of_wave in range(waves):
+        piece = meas_ref[of_wave, :, pl.ds(pl.multiple_of(sec * span, span), span)].T
+        for part in range(group // sections):
+            meas_out[of_wave, part] = piece[part * lines:(part + 1) * lines]
+
+    def meas_push(act):
+        for of_wave in range(waves):
+            for part in range(group // sections):
+                to = place(of_wave, sec * (group // sections) + part)
+                src = meas_out.at[of_wave, part]
+                if act:
+                    push(src, meas_in.at[row], meas_sem.at[0], meas_sem.at[1], *to)
+                else:
+                    settle(src, meas_sem.at[0], *to)
+
+    meas_push(True)
+
+    def circ_pass():
+        x = [
+            jnp.concatenate(
+                [state[:, b * chunk:(b + 1) * chunk],
+                 state[:, half + b * chunk:half + (b + 1) * chunk]], axis=1)
+            for b in range(4)
+        ]
+        sum_a, dif_a = x[0] + x[2], x[0] - x[2]
+        sum_b, dif_b = x[1] + x[3], times_i(x[1] - x[3])
+        folded = (sum_a + sum_b, dif_a - dif_b, sum_a - sum_b, dif_a + dif_b)
+        y = [complex_dot(folded[t], circ_h[t], circ_l[t]) for t in range(4)]
+        sum_a, dif_a = y[0] + y[2], y[0] - y[2]
+        sum_b, dif_b = y[1] + y[3], times_i(y[1] - y[3])
+        for b, value in enumerate((sum_a + sum_b, dif_a + dif_b, sum_a - sum_b, dif_a - dif_b)):
+            state[:, b * chunk:(b + 1) * chunk] = value[:, :chunk]
+            state[:, half + b * chunk:half + (b + 1) * chunk] = value[:, chunk:]
+
+    def to_freq():
+        even = complex_dot(state[:, :half], dft_h[0], dft_l[0])
+        odd = complex_dot(state[:, half:], dft_h[1], dft_l[1])
+        state[:, :half] = even + odd
+        state[:, half:] = even - odd
+
+    def from_freq():
+        first, second = state[:, :half], state[:, half:]
+        state[:, :half] = complex_dot(first + second, dft_h[0], dft_l[0])
+        state[:, half:] = complex_dot(first - second, dft_h[2], dft_l[2])
+
+    pair = 2 * lines
+
+    def exchange(step):
+        for block in range(width // pair):
+            turned = state[:, block * pair:(block + 1) * pair].T
+            send[step, 2 * block] = turned[:lines]
+            send[step, 2 * block + 1] = turned[lines:]
+
+        def start(count, carry):
+            other = (mine + count) % group
+            to_sec, to_row = place(wave, other)
+            pltpu.make_async_remote_copy(
+                src_ref=send.at[step, other], dst_ref=recv.at[step, mine],
+                send_sem=send_sem.at[step], recv_sem=recv_sem.at[step],
+                device_id=(to_sec, to_row), device_id_type=pl.DeviceIdType.MESH,
+            ).start()
+            return carry
+
+        lax.fori_loop(1, group, start, 0)
+        recv[step, mine] = send[step, mine]
+        arrived = recv.at[step, pl.ds(0, group - 1)]
+        pltpu.make_async_copy(arrived, arrived, recv_sem.at[step]).wait()
+        low = lax.broadcasted_iota(jnp.int32, (lines, pair), 1) < lines
+        for block in range(width // pair):
+            one, two = recv[step, 2 * block], recv[step, 2 * block + 1]
+            cols = slice(block * pair, (block + 1) * pair)
+            state[:lines, cols] = jnp.where(low, one, pltpu.roll(two, lines, 1))
+            state[lines:, cols] = jnp.where(low, pltpu.roll(one, lines, 1), two)
+
+    def wait_object(layer):
+        if layer % 2 == 0:
+            buf = obj_row.at[layer // 2]
+        else:
+            buf = obj_col.at[layer // 2]
+        pltpu.make_async_copy(buf, buf, obj_sem.at[layer]).wait()
+
+    def times_object(layer):
+        for r in range(rows):
+            cols = slice(r * shard, (r + 1) * shard)
+            if layer % 2 == 0:
+                o_re, o_im = obj_row[layer // 2, 0, :, cols], obj_row[layer // 2, 1, :, cols]
+            else:
+                o_re = obj_col[layer // 2, r, :, :shard]
+                o_im = obj_col[layer // 2, r, :, shard:]
+            re, im = state[:lines, cols], state[lines:, cols]
+            state[:lines, cols] = o_re * re - o_im * im
+            state[lines:, cols] = o_re * im + o_im * re
+
+    def grad_push(layer, act):
+        if layer % 2 == 0:
+            to = (layer, mine // per)
+            dst = grad_row.at[wave, mine % per]
+            src = grad_out.at[layer]
+            if act:
+                push(src, dst, grad_send.at[layer], grad_sem.at[0], *to)
+            else:
+                settle(src, grad_send.at[layer], *to)
+        else:
+            for r in range(rows):
+                src = grad_out.at[layer, :, :, pl.ds(r * shard, shard)]
+                dst = grad_col.at[wave, mine, :, :, :]
+                if act:
+                    push(src, dst, grad_send.at[layer], grad_sem.at[0], layer, r)
+                else:
+                    settle(src, grad_send.at[layer], layer, r)
+
+    def gradient(layer):
+        for r in range(rows):
+            cols = slice(r * shard, (r + 1) * shard)
+            re, im = state[:lines, cols], state[lines:, cols]
+            k_re, k_im = kept[layer, :lines, cols], kept[layer, lines:, cols]
+            grad_out[layer, 0, :, cols] = re * k_re - im * k_im
+            grad_out[layer, 1, :, cols] = -(re * k_im + im * k_re)
+        grad_push(layer, True)
+
+    pltpu.make_async_copy(spec_in, spec_in, spec_sem.at[1]).wait()
+    y_re, y_im = ramp_y[0], ramp_y[1]
+    x_re, x_im = ramp_x[0], ramp_x[1]
+    turn_re = x_re * y_re - x_im * y_im
+    turn_im = x_re * y_im + x_im * y_re
+    p_re, p_im = spec_in[0], spec_in[1]
+    state[:lines] = p_re * turn_re + p_im * turn_im
+    state[lines:] = p_re * turn_im - p_im * turn_re
+    from_freq()
+    exchange(0)
+    from_freq()
+    state[lines:] = -state[lines:]
+    for layer in range(layers):
+        kept[layer] = state[...]
+        wait_object(layer)
+        times_object(layer)
+        if layer + 1 < layers:
+            circ_pass()
+            exchange(1 + layer)
+            circ_pass()
+    to_freq()
+    exchange(layers)
+    to_freq()
+    pltpu.make_async_copy(meas_in, meas_in, meas_sem.at[1]).wait()
+    for r in range(rows):
+        cols = slice(r * shard, (r + 1) * shard)
+        re, im = state[:lines, cols], state[lines:, cols]
+        weight = 0.5 * (re * re + im * im - meas_in[r])
+        state[:lines, cols] = weight * re
+        state[lines:, cols] = -(weight * im)
+    from_freq()
+    exchange(layers + 1)
+    from_freq()
+    for layer in reversed(range(layers)):
+        gradient(layer)
+        if layer > 0:
+            times_object(layer)
+            circ_pass()
+            exchange(layers + 1 + layers - layer)
+            circ_pass()
+
+    settle(spec_src, spec_sem.at[0], *spec_to)
+    meas_push(False)
+    for layer in range(layers):
+        grad_push(layer, False)
+
+        @pl.when(sec == layer)
+        def _(layer=layer):
+            if layer % 2 == 0:
+                obj_row_push(layer, False)
+            else:
+                obj_col_push(layer, False)
+    for step in range(2 * layers + 1):
+        gone = send.at[step, pl.ds(0, group - 1)]
+        pltpu.make_async_copy(gone, gone, send_sem.at[step]).wait()
+
+    @pl.when(sec % 2 == 0)
+    def _():
+        pltpu.make_async_copy(grad_row, grad_row, grad_sem.at[0]).wait()
+        for part in range(per):
+            value = grad_row[0, part]
+            for of_wave in range(1, waves):
+                value = value + grad_row[of_wave, part]
+            out_ref[:, part * lines:(part + 1) * lines] = value
+
+    @pl.when(sec % 2 == 1)
+    def _():
+        pltpu.make_async_copy(grad_col, grad_col, grad_sem.at[0]).wait()
+        for block in range(width // pair):
+            for part in range(2):
+                pieces = []
+                for member in (2 * block, 2 * block + 1):
+                    value = grad_col[0, member, part]
+                    for of_wave in range(1, waves):
+                        value = value + grad_col[of_wave, member, part]
+                    pieces.append(value)
+                out_ref[part, :, block * pair:(block + 1) * pair] = jnp.concatenate(pieces, axis=0).T
+
+
+def fused_shards(object_slices, probe_spec, offsets, measured):
+    sections, rows = lax.axis_size("section"), lax.axis_size("row")
+    width = object_slices.shape[3]
+    waves = offsets.shape[0]
+    layers = sections * object_slices.shape[0]
+    dims = (sections, rows, waves, layers, width)
+    wave_rows = rows // waves
+    group = sections * wave_rows
+    lines = width // group
+    shard = width // rows
+    row = lax.axis_index("row")
+    mine = (row % wave_rows) * sections + lax.axis_index("section")
+    shift = lax.dynamic_index_in_dim(offsets, row // wave_rows, 0, keepdims=False)
+    unit = 2.0 * math.pi / width
+    turn_y = unit * (jnp.arange(width, dtype=jnp.int32) * shift[0] % width).astype(jnp.float32)
+    line = mine * lines + jnp.arange(lines, dtype=jnp.int32)
+    turn_x = unit * (line * shift[1] % width).astype(jnp.float32)
+    ramp_y = jnp.stack([jnp.cos(turn_y), jnp.sin(turn_y)])[:, None, :]
+    ramp_x = jnp.stack([jnp.cos(turn_x), jnp.sin(turn_x)])[:, :, None]
+    tables = [jnp.asarray(t) for t in fused_tables(width)]
+    steps = 2 * layers + 1
+    f32 = jnp.float32
+    vmem = pl.BlockSpec(memory_space=pltpu.VMEM)
+    even, odd = (layers + 1) // 2, layers // 2
+    dma = pltpu.SemaphoreType.DMA
+    result = pl.pallas_call(
+        lambda *refs: fused_kernel(dims, *refs),
+        out_shape=jax.ShapeDtypeStruct((2, shard, width), f32),
+        in_specs=[vmem] * 9,
+        out_specs=vmem,
+        scratch_shapes=[
+            pltpu.VMEM((2 * lines, width), f32),
+            pltpu.VMEM((steps, group, lines, 2 * lines), f32),
+            pltpu.VMEM((steps, group, lines, 2 * lines), f32),
+            pltpu.VMEM((2, lines, width), f32),
+            pltpu.VMEM((waves, group // sections, lines, shard), f32),
+            pltpu.VMEM((rows, lines, shard), f32),
+            pltpu.VMEM((group, lines, 2 * shard), f32),
+            pltpu.VMEM((even, 2, lines, width), f32),
+            pltpu.VMEM((odd, rows, lines, 2 * shard), f32),
+            pltpu.VMEM((layers, 2 * lines, width), f32),
+            pltpu.VMEM((layers, 2, lines, width), f32),
+            pltpu.VMEM((waves, shard // lines, 2, lines, width), f32),
+            pltpu.VMEM((waves, group, 2, lines, shard), f32),
+            dma((steps,)),
+            dma((steps,)),
+            dma((2,)),
+            dma((2,)),
+            dma((1,)),
+            dma((layers,)),
+            dma((layers,)),
+            dma((1,)),
+        ],
+        compiler_params=pltpu.CompilerParams(
+            collective_id=0, has_side_effects=True, vmem_limit_bytes=60 * 1024 * 1024
+        ),
+    )(object_slices[0], probe_spec, measured, ramp_y, ramp_x, *tables)
+    return result[None]
+
+
+def fused_fits(sections, rows, waves, layers, width):
+    if rows % waves or layers != sections or layers % 2:
+        return False
+    group = sections * rows // waves
+    if width % group or width % rows or group % sections:
+        return False
+    lines, shard = width // group, width // rows
+    if 2 * lines != 128 or shard != 2 * lines or width % 1024:
+        return False
+    return sections == waves * (shard // lines)
+
+
 def solution(mesh):
     placed = (P("section", None, "row", None), P(None, "row", None), P(), P(None, "row", None))
-    return jax.shard_map(
-        shards,
-        mesh=mesh,
-        in_specs=placed,
-        out_specs=P("section", None, "row", None),
-        check_vma=False,
-    )
+
+    def build(body):
+        return jax.shard_map(
+            body,
+            mesh=mesh,
+            in_specs=placed,
+            out_specs=P("section", None, "row", None),
+            check_vma=False,
+        )
+
+    def run(object_slices, probe_spec, offsets, measured):
+        fits = fused_fits(
+            mesh.shape["section"], mesh.shape["row"], offsets.shape[0],
+            object_slices.shape[0], object_slices.shape[3],
+        )
+        body = fused_shards if fits else shards
+        return build(body)(object_slices, probe_spec, offsets, measured)
+
+    return run

time: 954 us -> 236 us (0.25); the launches traced: 939 us -> 236 us
  blocking collectives: 234 us -> 0 us
  Pallas kernels: 0 us -> 229 us
  local copies, waits for them, and re-layouts: 226 us -> 4.93 us
  waiting for transfers between devices: 211 us -> 0 us
  matrix products: 111 us -> 0 us
  other arithmetic: 103 us -> 1.47 us
  starting transfers between devices: 38.5 us -> 0 us
  between operations: 15.4 us -> 0.03 us
    all_to_all x8 -> x0, blocking collectives: 234 us -> none  [the longest x5 146 us: transform_forward(): lax.all_to_all(partial_out, 'row', split_axis=3, concat_axis=2, tiled=True)]
    pallas_call x0 -> x1, Pallas kernels: none -> 229 us  [fused_shards(): pl.pallas_call(lambda *refs: fused_kernel(dims, *refs), out_shape=jax.Sha...]
    all_to_all x7 -> x0, waiting for transfers between devices: 159 us -> none  [the longest x5 110 us: transform_inverse(): lax.all_to_all(partial_out, 'row', split_axis=3, concat_axis=2, tiled=True)]
    dot_general x30 -> x0, matrix products: 111 us -> none  [the longest x15 53.8 us: small_dft(): result = jnp.dot(flat, both_tables, precision=highest)]
    all_to_all x30 -> x0, local copies, waits for them, and re-layouts: 54.5 us -> none  [the longest x16 30.8 us: transform_inverse(): lax.all_to_all(partial_out, 'row', split_axis=3, concat_axis=2, tiled=True)]
    unnamed x3 -> x0, waiting for transfers between devices: 52.5 us -> none
    all_to_all x7 -> x0, starting transfers between devices: 38.5 us -> none  [the longest x5 27.9 us: transform_inverse(): lax.all_to_all(partial_out, 'row', split_axis=3, concat_axis=2, tiled=True)]
    another operation x75 -> x1, other arithmetic: 34.2 us -> 0.01 us  [fused_shards(): ramp_y = jnp.stack([jnp.cos(turn_y), jnp.sin(turn_y)])[:, None, :]]
  transfers between devices with their start and end apart: 9 -> 0, of which waited for: 8 -> 0; matrix products, arithmetic and copies ran while one was open for 6% -> 0% of each run, Pallas kernels for 0% -> 0%
where the time goes in v1:
time: 236 us
  Pallas kernels  229 us (97%)
  local copies, waits for them, and re-layouts  4.93 us (2%)
    pallas_call x1, Pallas kernels, fused_shards(): pl.pallas_call(lambda *refs: fused_kernel(dims, *refs), out_shape=jax.Sha...  229 us

profile of v1, /device:TPU:1, one launch (start us, length us, event | category | flops | bytes accessed | tf_op | source)
XLA Modules:
  0.0 235.7 jit_solution(7699041637701449671)
XLA Ops:
  0.0 0.0 copy-start
  0.0 0.7 copy-done
  0.7 0.6 fusion.10
  1.3 0.7 fusion.8
  2.0 0.8 fusion.3
  2.8 0.6 broadcast_in_dim.9.refs_3_
  3.4 0.7 copy.9.refs_4_
  4.1 229.3 %shard_map.82 = f32[2,128,1024]{2,1,0:T(8,128)} custom-call(f32[2,128,1024]{2,1,0:T(8,128)} %bitcast.7, f32[2,128,1024]{2,1,0:T(8,128)} %refs_1_.1, f32[2,128,1024]{2,1,0:T(8,128)} %refs_2_.1, f32[2,1,1024]{2,1,0:T(1,128)} %broadcast_in_dim.9.refs_3_, f32[2,64,1]{2,1,0:T(8,128)} %copy.9.refs_4_, bf16[4,256,512]{2,1,0:T(8,128)(2,1)} %constant.73.clone.refs_5_, ...), custom_call_target="tpu_custom_call" | custom-call | tf_op jit(solution)/shard_map/pallas_call | solution.py:567
  233.4 2.3 copy.11
  (3 shorter events, 0.0 us)
Async XLA Ops:
  0.0 0.7 copy-start

commit v2 on v1

--- a/solution.py
+++ b/solution.py
@@ -238,21 +238,23 @@
 
 def fused_kernel(
     dims, obj_ref, spec_ref, meas_ref, ramp_y, ramp_x, circ_h, circ_l, dft_h, dft_l, out_ref,
-    state, send, recv, spec_in, meas_out, meas_in, obj_out, obj_row, obj_col, kept, grad_out,
-    grad_row, grad_col, send_sem, recv_sem, spec_sem, meas_sem, obj_send, obj_sem, grad_send,
-    grad_sem,
+    state, send, recv, spec_in, meas_out, meas_in, obj_out, obj_hop, obj_row, obj_col, kept,
+    grad_out, grad_hop, grad_sum, grad_row, grad_col, send_sem, recv_sem, spec_sem, meas_sem,
+    obj_send, hop_sem, obj_sem, pair_sem, fold_sem, grad_send, grad_sem,
 ):
     sections, rows, waves, layers, width = dims
     wave_rows = rows // waves
     group = sections * wave_rows
     lines = width // group
     shard = width // rows
-    per = shard // lines
+    piece = lines // 2
     half, chunk = width // 2, width // 8
+    even, odd = (layers + 1) // 2, layers // 2
     sec = lax.axis_index("section")
     row = lax.axis_index("row")
     wave = row // wave_rows
     mine = (row % wave_rows) * sections + sec
+    mate = wave_rows + row - 2 * wave_rows * wave
     total = sections * rows
     me = sec * rows + row
 
@@ -291,71 +293,81 @@
     lax.fori_loop(1, total, greet, 0)
     pl.semaphore_wait(barrier, total - 1)
 
-    spec_wave = sec // per
-    spec_part = sec % per
-    spec_to = place(spec_wave, row * per + spec_part)
-    spec_src = spec_ref.at[:, pl.ds(pl.multiple_of(spec_part * lines, lines), lines)]
-    push(spec_src, spec_in, spec_sem.at[0], spec_sem.at[1], *spec_to)
-
-    def obj_row_push(layer, act):
-        for part in range(per):
-            for of_wave in range(waves):
-                src = obj_ref.at[:, pl.ds(part * lines, lines)]
-                to = place(of_wave, row * per + part)
-                if act:
-                    push(src, obj_row.at[layer // 2], obj_send.at[0], obj_sem.at[layer], *to)
-                else:
-                    settle(src, obj_send.at[0], *to)
-
-    def obj_col_push(layer, act):
-        def step(count, carry):
-            member = count // waves
-            of_wave = count % waves
-            to = place(of_wave, member)
-            src = obj_out.at[member]
+    own = pl.ds(pl.multiple_of(sec * piece, piece), piece)
+    spec_src = spec_ref.at[:, own]
+    pltpu.make_async_copy(spec_src, spec_in.at[wave], spec_sem.at[2]).start()
+    push(spec_src, spec_in.at[wave], spec_sem.at[0], spec_sem.at[1], sec, mate)
+
+    def hop_src(layer, to_sec):
+        if layer % 2 == 0:
+            return obj_ref.at[:, pl.ds(to_sec * piece, piece)]
+        return obj_out.at[to_sec]
+
+    def hop_dst(layer):
+        if layer % 2 == 0:
+            return obj_row.at[layer // 2, wave]
+        return obj_hop.at[layer // 2]
+
+    def obj_first(layer, act):
+        for to_sec in range(sections):
             if act:
-                push(src, obj_col.at[layer // 2, row], obj_send.at[0], obj_sem.at[layer], *to)
+                push(hop_src(layer, to_sec), hop_dst(layer), obj_send.at[0], hop_sem.at[layer],
+                     to_sec, row)
             else:
-                settle(src, obj_send.at[0], *to)
-            return carry
-
-        lax.fori_loop(0, group * waves, step, 0)
+                settle(hop_src(layer, to_sec), obj_send.at[0], to_sec, row)
+
+    def obj_second(layer, act):
+        if layer % 2 == 0:
+            src = obj_row.at[layer // 2, wave]
+            if act:
+                pltpu.make_async_copy(src, src, hop_sem.at[layer]).wait()
+                push(src, src, obj_send.at[1 + layer], obj_sem.at[layer], sec, mate)
+            else:
+                settle(src, obj_send.at[1 + layer], sec, mate)
+            return
+        if act:
+            src = obj_hop.at[layer // 2]
+            pltpu.make_async_copy(src, src, hop_sem.at[layer]).wait()
+        for to_row in range(rows):
+            src = obj_hop.at[layer // 2, to_row % wave_rows]
+            if act:
+                push(src, obj_col.at[layer // 2, row], obj_send.at[1 + layer], obj_sem.at[layer],
+                     sec, to_row)
+            else:
+                settle(src, obj_send.at[1 + layer], sec, to_row)
 
     def transpose_obj():
-        for block in range(width // shard):
+        for block in range(rows):
             for part in range(2):
                 turned = obj_ref[part, :, block * shard:(block + 1) * shard].T
-                for piece in range(per):
-                    obj_out[block * per + piece, :, part * shard:(part + 1) * shard] = (
-                        turned[piece * lines:(piece + 1) * lines]
+                for to_sec in range(sections):
+                    obj_out[to_sec, block % wave_rows, block // wave_rows, :,
+                            part * shard:(part + 1) * shard] = (
+                        turned[to_sec * piece:(to_sec + 1) * piece]
                     )
 
     for layer in range(layers):
         @pl.when(sec == layer)
         def _(layer=layer):
-            if layer % 2 == 0:
-                obj_row_push(layer, True)
-            else:
+            if layer % 2 == 1:
                 transpose_obj()
-                obj_col_push(layer, True)
-
-    span = width // sections
-    for of_wave in range(waves):
-        piece = meas_ref[of_wave, :, pl.ds(pl.multiple_of(sec * span, span), span)].T
-        for part in range(group // sections):
-            meas_out[of_wave, part] = piece[part * lines:(part + 1) * lines]
+            obj_first(layer, True)
 
     def meas_push(act):
+        for to_row in range(rows):
+            for side in range(2):
+                src = meas_out.at[to_row // wave_rows, to_row % wave_rows + side * wave_rows, own]
+                dst = meas_in.at[row, pl.ds(side * piece, piece)]
+                if act:
+                    push(src, dst, meas_sem.at[0], meas_sem.at[1], sec, to_row)
+                else:
+                    settle(src, meas_sem.at[0], sec, to_row)
+
+    def turn_meas():
         for of_wave in range(waves):
-            for part in range(group // sections):
-                to = place(of_wave, sec * (group // sections) + part)
-                src = meas_out.at[of_wave, part]
-                if act:
-                    push(src, meas_in.at[row], meas_sem.at[0], meas_sem.at[1], *to)
-                else:
-                    settle(src, meas_sem.at[0], *to)
-
-    meas_push(True)
+            for block in range(rows):
+                meas_out[of_wave, block] = meas_ref[of_wave, :, block * shard:(block + 1) * shard].T
+        meas_push(True)
 
     def circ_pass():
         x = [
@@ -387,11 +399,14 @@
 
     pair = 2 * lines
 
-    def exchange(step):
-        for block in range(width // pair):
+    def exchange(step, meanwhile=lambda: None):
+        for block in range(rows):
             turned = state[:, block * pair:(block + 1) * pair].T
-            send[step, 2 * block] = turned[:lines]
-            send[step, 2 * block + 1] = turned[lines:]
+            side = (block // wave_rows) * piece
+            for part in range(sections):
+                send[step, (block % wave_rows) * sections + part, side:side + piece] = (
+                    turned[part * piece:(part + 1) * piece]
+                )
 
         def start(count, carry):
             other = (mine + count) % group
@@ -405,18 +420,25 @@
 
         lax.fori_loop(1, group, start, 0)
         recv[step, mine] = send[step, mine]
+        meanwhile()
         arrived = recv.at[step, pl.ds(0, group - 1)]
         pltpu.make_async_copy(arrived, arrived, recv_sem.at[step]).wait()
-        low = lax.broadcasted_iota(jnp.int32, (lines, pair), 1) < lines
-        for block in range(width // pair):
-            one, two = recv[step, 2 * block], recv[step, 2 * block + 1]
-            cols = slice(block * pair, (block + 1) * pair)
-            state[:lines, cols] = jnp.where(low, one, pltpu.roll(two, lines, 1))
-            state[lines:, cols] = jnp.where(low, pltpu.roll(one, lines, 1), two)
+        spot = lax.broadcasted_iota(jnp.int32, (lines, pair), 1) // piece
+        for block in range(wave_rows):
+            tiles = [recv[step, block * sections + part] for part in range(sections)]
+            for which in range(4):
+                out = None
+                for part in range(sections):
+                    turn = (part - which) % 4 * piece
+                    moved = pltpu.roll(tiles[part], turn, 1) if turn else tiles[part]
+                    out = moved if out is None else jnp.where(spot == part, moved, out)
+                first = (which // 2) * lines
+                col = (block + which % 2 * wave_rows) * pair
+                state[first:first + lines, col:col + pair] = out
 
     def wait_object(layer):
         if layer % 2 == 0:
-            buf = obj_row.at[layer // 2]
+            buf = obj_row.at[layer // 2, 0]
         else:
             buf = obj_col.at[layer // 2]
         pltpu.make_async_copy(buf, buf, obj_sem.at[layer]).wait()
@@ -425,31 +447,57 @@
         for r in range(rows):
             cols = slice(r * shard, (r + 1) * shard)
             if layer % 2 == 0:
-                o_re, o_im = obj_row[layer // 2, 0, :, cols], obj_row[layer // 2, 1, :, cols]
+                o_re, o_im = (
+                    jnp.concatenate([obj_row[layer // 2, side, part, :, cols] for side in range(2)], axis=0)
+                    for part in range(2)
+                )
             else:
-                o_re = obj_col[layer // 2, r, :, :shard]
-                o_im = obj_col[layer // 2, r, :, shard:]
+                both = jnp.concatenate([obj_col[layer // 2, r, side] for side in range(2)], axis=0)
+                o_re, o_im = both[:, :shard], both[:, shard:]
             re, im = state[:lines, cols], state[lines:, cols]
             state[:lines, cols] = o_re * re - o_im * im
             state[lines:, cols] = o_re * im + o_im * re
 
-    def grad_push(layer, act):
+    def fold_src(layer):
         if layer % 2 == 0:
-            to = (layer, mine // per)
-            dst = grad_row.at[wave, mine % per]
-            src = grad_out.at[layer]
+            return grad_out.at[layer, :, pl.ds(pl.multiple_of((1 - wave) * piece, piece), piece)]
+        return grad_out.at[layer, :, :, pl.ds(pl.multiple_of((1 - wave) * half, half), half)]
+
+    def fold_dst(layer):
+        if layer % 2 == 0:
+            return grad_hop.at[layer // 2]
+        return grad_sum.at[layer // 2]
+
+    def grad_first(layer):
+        push(fold_src(layer), fold_dst(layer), pair_sem.at[layer], fold_sem.at[layer], sec, mate)
+
+    def last_push(layer, act):
+        if layer % 2 == 0:
+            src = grad_hop.at[even + layer // 2]
             if act:
-                push(src, dst, grad_send.at[layer], grad_sem.at[0], *to)
+                push(src, grad_row.at[sec], grad_send.at[layer], grad_sem.at[0], layer, row)
             else:
-                settle(src, grad_send.at[layer], *to)
+                settle(src, grad_send.at[layer], layer, row)
+            return
+        for part in range(wave_rows):
+            to_row = wave * wave_rows + part
+            src = grad_sum.at[odd + layer // 2, :, :, pl.ds(part * shard, shard)]
+            dst = grad_col.at[row % wave_rows, sec]
+            if act:
+                push(src, dst, grad_send.at[layer], grad_sem.at[0], layer, to_row)
+            else:
+                settle(src, grad_send.at[layer], layer, to_row)
+
+    def grad_second(layer):
+        came = fold_dst(layer)
+        pltpu.make_async_copy(came, came, fold_sem.at[layer]).wait()
+        if layer % 2 == 0:
+            held = grad_out[layer, :, pl.ds(pl.multiple_of(wave * piece, piece), piece)]
+            grad_hop[even + layer // 2] = grad_hop[layer // 2] + held
         else:
-            for r in range(rows):
-                src = grad_out.at[layer, :, :, pl.ds(r * shard, shard)]
-                dst = grad_col.at[wave, mine, :, :, :]
-                if act:
-                    push(src, dst, grad_send.at[layer], grad_sem.at[0], layer, r)
-                else:
-                    settle(src, grad_send.at[layer], layer, r)
+            held = grad_out[layer, :, :, pl.ds(pl.multiple_of(wave * half, half), half)]
+            grad_sum[odd + layer // 2] = grad_sum[layer // 2] + held
+        last_push(layer, True)
 
     def gradient(layer):
         for r in range(rows):
@@ -458,18 +506,26 @@
             k_re, k_im = kept[layer, :lines, cols], kept[layer, lines:, cols]
             grad_out[layer, 0, :, cols] = re * k_re - im * k_im
             grad_out[layer, 1, :, cols] = -(re * k_im + im * k_re)
-        grad_push(layer, True)
-
-    pltpu.make_async_copy(spec_in, spec_in, spec_sem.at[1]).wait()
+
+    pltpu.make_async_copy(spec_in.at[0], spec_in.at[0], spec_sem.at[1]).wait()
+    pltpu.make_async_copy(spec_in.at[0], spec_in.at[0], spec_sem.at[2]).wait()
     y_re, y_im = ramp_y[0], ramp_y[1]
     x_re, x_im = ramp_x[0], ramp_x[1]
     turn_re = x_re * y_re - x_im * y_im
     turn_im = x_re * y_im + x_im * y_re
-    p_re, p_im = spec_in[0], spec_in[1]
+    p_re, p_im = (
+        jnp.concatenate([spec_in[side, part] for side in range(2)], axis=0) for part in range(2)
+    )
     state[:lines] = p_re * turn_re + p_im * turn_im
     state[lines:] = p_re * turn_im - p_im * turn_re
     from_freq()
-    exchange(0)
+
+    def first_objects():
+        obj_second(0, True)
+        turn_meas()
+        obj_second(1, True)
+
+    exchange(0, first_objects)
     from_freq()
     state[lines:] = -state[lines:]
     for layer in range(layers):
@@ -478,7 +534,11 @@
         times_object(layer)
         if layer + 1 < layers:
             circ_pass()
-            exchange(1 + layer)
+            later = layer + 2
+            if later < layers:
+                exchange(1 + layer, lambda later=later: obj_second(later, True))
+            else:
+                exchange(1 + layer)
             circ_pass()
     to_freq()
     exchange(layers)
@@ -498,20 +558,29 @@
         if layer > 0:
             times_object(layer)
             circ_pass()
-            exchange(layers + 1 + layers - layer)
+
+            def gradients(layer=layer):
+                grad_first(layer)
+                if layer + 1 < layers:
+                    grad_second(layer + 1)
+
+            exchange(layers + 1 + layers - layer, gradients)
             circ_pass()
 
-    settle(spec_src, spec_sem.at[0], *spec_to)
+    grad_first(0)
+    grad_second(1)
+    grad_second(0)
+
+    settle(spec_src, spec_sem.at[0], sec, mate)
     meas_push(False)
     for layer in range(layers):
-        grad_push(layer, False)
+        settle(fold_src(layer), pair_sem.at[layer], sec, mate)
+        last_push(layer, False)
+        obj_second(layer, False)
 
         @pl.when(sec == layer)
         def _(layer=layer):
-            if layer % 2 == 0:
-                obj_row_push(layer, False)
-            else:
-                obj_col_push(layer, False)
+            obj_first(layer, False)
     for step in range(2 * layers + 1):
         gone = send.at[step, pl.ds(0, group - 1)]
         pltpu.make_async_copy(gone, gone, send_sem.at[step]).wait()
@@ -519,24 +588,19 @@
     @pl.when(sec % 2 == 0)
     def _():
         pltpu.make_async_copy(grad_row, grad_row, grad_sem.at[0]).wait()
-        for part in range(per):
-            value = grad_row[0, part]
-            for of_wave in range(1, waves):
-                value = value + grad_row[of_wave, part]
-            out_ref[:, part * lines:(part + 1) * lines] = value
+        for part in range(sections):
+            out_ref[:, part * piece:(part + 1) * piece] = grad_row[part]
 
     @pl.when(sec % 2 == 1)
     def _():
         pltpu.make_async_copy(grad_col, grad_col, grad_sem.at[0]).wait()
-        for block in range(width // pair):
+        for block in range(rows):
+            side = (block // wave_rows) * piece
             for part in range(2):
-                pieces = []
-                for member in (2 * block, 2 * block + 1):
-                    value = grad_col[0, member, part]
-                    for of_wave in range(1, waves):
-                        value = value + grad_col[of_wave, member, part]
-                    pieces.append(value)
-                out_ref[part, :, block * pair:(block + 1) * pair] = jnp.concatenate(pieces, axis=0).T
+                joined = jnp.concatenate(
+                    [grad_col[block % wave_rows, member, part, side:side + piece]
+                     for member in range(sections)], axis=0)
+                out_ref[part, :, block * pair:(block + 1) * pair] = joined.T
 
 
 def fused_shards(object_slices, probe_spec, offsets, measured):
@@ -550,11 +614,13 @@
     lines = width // group
     shard = width // rows
     row = lax.axis_index("row")
-    mine = (row % wave_rows) * sections + lax.axis_index("section")
     shift = lax.dynamic_index_in_dim(offsets, row // wave_rows, 0, keepdims=False)
     unit = 2.0 * math.pi / width
     turn_y = unit * (jnp.arange(width, dtype=jnp.int32) * shift[0] % width).astype(jnp.float32)
-    line = mine * lines + jnp.arange(lines, dtype=jnp.int32)
+    piece = lines // 2
+    inner = jnp.arange(lines, dtype=jnp.int32)
+    line = (row % wave_rows + wave_rows * (inner // piece)) * shard
+    line = line + lax.axis_index("section") * piece + inner % piece
     turn_x = unit * (line * shift[1] % width).astype(jnp.float32)
     ramp_y = jnp.stack([jnp.cos(turn_y), jnp.sin(turn_y)])[:, None, :]
     ramp_x = jnp.stack([jnp.cos(turn_x), jnp.sin(turn_x)])[:, :, None]
@@ -573,21 +639,27 @@
             pltpu.VMEM((2 * lines, width), f32),
             pltpu.VMEM((steps, group, lines, 2 * lines), f32),
             pltpu.VMEM((steps, group, lines, 2 * lines), f32),
-            pltpu.VMEM((2, lines, width), f32),
-            pltpu.VMEM((waves, group // sections, lines, shard), f32),
+            pltpu.VMEM((2, 2, piece, width), f32),
+            pltpu.VMEM((waves, rows, shard, shard), f32),
             pltpu.VMEM((rows, lines, shard), f32),
-            pltpu.VMEM((group, lines, 2 * shard), f32),
-            pltpu.VMEM((even, 2, lines, width), f32),
-            pltpu.VMEM((odd, rows, lines, 2 * shard), f32),
+            pltpu.VMEM((sections, wave_rows, 2, piece, 2 * shard), f32),
+            pltpu.VMEM((odd, wave_rows, 2, piece, 2 * shard), f32),
+            pltpu.VMEM((even, 2, 2, piece, width), f32),
+            pltpu.VMEM((odd, rows, 2, piece, 2 * shard), f32),
             pltpu.VMEM((layers, 2 * lines, width), f32),
             pltpu.VMEM((layers, 2, lines, width), f32),
-            pltpu.VMEM((waves, shard // lines, 2, lines, width), f32),
-            pltpu.VMEM((waves, group, 2, lines, shard), f32),
+            pltpu.VMEM((2 * even, 2, piece, width), f32),
+            pltpu.VMEM((2 * odd, 2, lines, width // 2), f32),
+            pltpu.VMEM((sections, 2, piece, width), f32),
+            pltpu.VMEM((wave_rows, sections, 2, lines, shard), f32),
             dma((steps,)),
             dma((steps,)),
+            dma((3,)),
             dma((2,)),
-            dma((2,)),
-            dma((1,)),
+            dma((1 + layers,)),
+            dma((layers,)),
+            dma((layers,)),
+            dma((layers,)),
             dma((layers,)),
             dma((layers,)),
             dma((1,)),
@@ -608,7 +680,7 @@
     lines, shard = width // group, width // rows
     if 2 * lines != 128 or shard != 2 * lines or width % 1024:
         return False
-    return sections == waves * (shard // lines)
+    return waves == 2 and sections == 4
 
 
 def solution(mesh):

time: 236 us -> 178 us (0.75)
  Pallas kernels: 229 us -> 171 us
    pallas_call x1, Pallas kernels: 229 us -> 171 us  [fused_shards(): pl.pallas_call(lambda *refs: fused_kernel(dims, *refs), out_shape=jax.Sha...]
where the time goes in v2:
time: 178 us; the launch traced here: 177 us
  Pallas kernels  171 us (96%)
  local copies, waits for them, and re-layouts  4.93 us (3%)
    pallas_call x1, Pallas kernels, fused_shards(): pl.pallas_call(lambda *refs: fused_kernel(dims, *refs), out_shape=jax.Sha...  171 us

profile of v2, /device:TPU:1, one launch (start us, length us, event | category | flops | bytes accessed | tf_op | source)
XLA Modules:
  0.0 177.0 jit_solution(12456154829940397591)
XLA Ops:
  0.0 0.0 copy-start
  0.0 0.7 copy-done
  0.7 0.6 fusion.16
  1.3 0.7 fusion.14
  2.0 0.8 fusion.3
  2.8 0.6 broadcast_in_dim.9.refs_3_
  3.4 0.7 copy.9.refs_4_
  4.1 170.6 %shard_map.82 = f32[2,128,1024]{2,1,0:T(8,128)} custom-call(f32[2,128,1024]{2,1,0:T(8,128)} %bitcast.7, f32[2,128,1024]{2,1,0:T(8,128)} %refs_1_.1, f32[2,128,1024]{2,1,0:T(8,128)} %refs_2_.1, f32[2,1,1024]{2,1,0:T(1,128)} %broadcast_in_dim.9.refs_3_, f32[2,64,1]{2,1,0:T(8,128)} %copy.9.refs_4_, bf16[4,256,512]{2,1,0:T(8,128)(2,1)} %constant.101.clone.refs_5_, ...), custom_call_target="tpu_custom_call" | custom-call | tf_op jit(solution)/shard_map/pallas_call | solution.py:633
  174.7 2.3 %copy.11 = f32[1,2,128,1024]{3,2,1,0:T(8,128)} copy(f32[1,2,128,1024]{3,2,1,0:T(8,128)} %bitcast.6) | data formatting | bytes 2097152
  (3 shorter events, 0.0 us)
Async XLA Ops:
  0.0 0.7 copy-start

commit v3 on v2

--- a/solution.py
+++ b/solution.py
@@ -409,8 +409,12 @@
                 )
 
         def start(count, carry):
-            other = (mine + count) % group
-            to_sec, to_row = place(wave, other)
+            code = group - count
+            spot = row % wave_rows
+            to_sec = (sec // 2 + code // 4) % 2 * 2 + (sec + code // 2) % 2
+            to_spot = (spot // 2 + code // 8) % 2 * 2 + (spot + code) % 2
+            to_row = wave * wave_rows + to_spot
+            other = to_spot * sections + to_sec
             pltpu.make_async_remote_copy(
                 src_ref=send.at[step, other], dst_ref=recv.at[step, mine],
                 send_sem=send_sem.at[step], recv_sem=recv_sem.at[step],
@@ -680,7 +684,7 @@
     lines, shard = width // group, width // rows
     if 2 * lines != 128 or shard != 2 * lines or width % 1024:
         return False
-    return waves == 2 and sections == 4
+    return waves == 2 and sections == 4 and rows == 8
 
 
 def solution(mesh):

time: 178 us -> 179 us (level)
  no operation moved by 1% of the time
where the time goes in v3:
time: 179 us; the launch traced here: 178 us
  Pallas kernels  172 us (96%)
  local copies, waits for them, and re-layouts  4.93 us (3%)
    pallas_call x1, Pallas kernels, fused_shards(): pl.pallas_call(lambda *refs: fused_kernel(dims, *refs), out_shape=jax.Sha...  172 us

profile of v3, /device:TPU:1, one launch (start us, length us, event | category | flops | bytes accessed | tf_op | source)
XLA Modules:
  0.0 178.1 jit_solution(16414816239586445602)
XLA Ops:
  0.0 0.0 copy-start
  0.0 0.7 copy-done
  0.7 0.6 fusion.16
  1.3 0.7 fusion.14
  2.0 0.8 fusion.3
  2.8 0.6 broadcast_in_dim.9.refs_3_
  3.4 0.7 copy.9.refs_4_
  4.1 171.7 %shard_map.82 = f32[2,128,1024]{2,1,0:T(8,128)} custom-call(f32[2,128,1024]{2,1,0:T(8,128)} %bitcast.7, f32[2,128,1024]{2,1,0:T(8,128)} %refs_1_.1, f32[2,128,1024]{2,1,0:T(8,128)} %refs_2_.1, f32[2,1,1024]{2,1,0:T(1,128)} %broadcast_in_dim.9.refs_3_, f32[2,64,1]{2,1,0:T(8,128)} %copy.9.refs_4_, bf16[4,256,512]{2,1,0:T(8,128)(2,1)} %constant.101.clone.refs_5_, ...), custom_call_target="tpu_custom_call" | custom-call | tf_op jit(solution)/shard_map/pallas_call | solution.py:637
  175.8 2.3 %copy.11 = f32[1,2,128,1024]{3,2,1,0:T(8,128)} copy(f32[1,2,128,1024]{3,2,1,0:T(8,128)} %bitcast.6) | data formatting | bytes 2097152
  (3 shorter events, 0.0 us)
Async XLA Ops:
  0.0 0.7 copy-start
